TPU v7x, 256 devices: a whole 4x4x8 slice. The times are simulated.
256 devices in a mesh: comp: 2 (over x_lo), ox: 16 (over x_hi, y, core), oy: 8 (over z).
Axes of the slice: x: 4 (x_hi: 2, x_lo: 2; x = x_hi * 2 + x_lo), y: 4, z: 8, core: 2. Of those that a mesh axis runs over, the one named last changes fastest.
Arguments:
- atmos_stress: float32 [2, 2359296], P(None, ('comp', 'ox', 'oy')), may hold values from -6 to 6
- route_tile: int32 [2359296, 1], P(('comp', 'ox', 'oy')), may hold values from 0 to 255; in each aligned block of 9216 rows (0 to 9215, 9216 to 18431, ...) at most 144 rows name the same one
- route_cell: int32 [2359296], P(('comp', 'ox', 'oy')), may hold values from 0 to 54674
- route_weight: float32 [2359296], P(('comp', 'ox', 'oy')), may hold values from 0.25 to 1
- velocity: float32 [2, 8, 4320, 3240], P(None, None, ('comp', 'ox'), 'oy'), may hold values from -6 to 6
- thickness: float32 [8, 4320, 3240], P(None, ('comp', 'ox'), 'oy'), may hold values from 0.5 to 2
- coriolis: float32 [4320, 3240], P(('comp', 'ox'), 'oy'), may hold values from -0.5 to 0.5
- ocean_axes: float32 [2, 3, 4320, 3240], P(None, None, ('comp', 'ox'), 'oy'), may hold values from -3 to 3
- ocean_mask: int32 [4320, 3240], P(('comp', 'ox'), 'oy'), may hold values 0 or 1
Outputs:
- new_velocity: float32 [2, 8, 4320, 3240], P(None, None, ('comp', 'ox'), 'oy')
Inputs may be any that keep to these rules, and one draw needn't show every extreme that they name: `route_tile`: tiles are numbered as devices, comp-major, then ox, then oy. Of the 9216 cells of one device, at most 144 name the same tile, and on some device exactly 144 do.
All inputs are finite; a program needn't handle non-finite values. No bound on the sum of `ocean_mask` on one device may be relied on, other than what follows from the above.
Results may differ from a plain program's by a relative error of at most 0.0003.
Values sent between devices are 32-bit elements; how exact they have to be, the bound alone decides.
A program may use at most 128 MiB of HBM per device.

v0:
```python
import math
import jax
import jax.numpy as jnp
import numpy as np
from jax import lax
from jax.sharding import PartitionSpec as P

A_ROWS = 48
A_COLS = 64
face_normal = np.array(
    [[1.0, 0, 0], [0, 1.0, 0], [-1.0, 0, 0], [0, -1.0, 0], [0, 0, 1.0], [0, 0, -1.0]]
)
face_first = np.array(
    [[0, 1.0, 0], [-1.0, 0, 0], [0, -1.0, 0], [1.0, 0, 0], [0, 1.0, 0], [0, 1.0, 0]]
)
face_second = np.array(
    [[0, 0, 1.0], [0, 0, 1.0], [0, 0, 1.0], [0, 0, 1.0], [-1.0, 0, 0], [1.0, 0, 0]]
)
viscosity = 0.2
coupling = 0.3
bottom_drag = 0.1


def extended(block, sides, width, periodic):
    for axis, dim in sides:
        count = lax.axis_size(axis)
        forward = [(i, i + 1) for i in range(count - 1)]
        if periodic:
            forward.append((count - 1, 0))
        backward = [(target, source) for source, target in forward]
        low = lax.ppermute(
            lax.slice_in_dim(block, block.shape[dim] - width, None, axis=dim), axis, forward
        )
        high = lax.ppermute(lax.slice_in_dim(block, 0, width, axis=dim), axis, backward)
        block = jnp.concatenate([low, block, high], axis=dim)
    return block


def frame_rows(face_table, face_id):
    face_numbers = jnp.arange(6, dtype=jnp.int32)
    face_hits = (face_id[None, :] == face_numbers[:, None]).astype(jnp.float32)
    return jnp.dot(
        jnp.asarray(face_table.T, dtype=jnp.float32), face_hits, precision=lax.Precision.HIGHEST
    )


def tangent(direction, radial):
    projected = direction - jnp.sum(direction * radial, axis=0, keepdims=True) * radial
    return projected / jnp.sqrt(jnp.sum(projected * projected, axis=0, keepdims=True))


def cartesian(stress, face_id, cell_row, cell_col, cube_rows, cube_cols):
    normal = frame_rows(face_normal, face_id)
    first_axis = frame_rows(face_first, face_id)
    second_axis = frame_rows(face_second, face_id)
    slant_row = jnp.tan(
        (cell_row.astype(jnp.float32) + 0.5) * (0.5 * math.pi / cube_rows) - 0.25 * math.pi
    )
    slant_col = jnp.tan(
        (cell_col.astype(jnp.float32) + 0.5) * (0.5 * math.pi / cube_cols) - 0.25 * math.pi
    )
    surface_point = normal + slant_row[None, :] * first_axis + slant_col[None, :] * second_axis
    radial = surface_point / jnp.sqrt(jnp.sum(surface_point * surface_point, axis=0, keepdims=True))
    return stress[0][None, :] * tangent(first_axis, radial) + stress[1][None, :] * tangent(
        second_axis, radial
    )


def advance(masked, east, west, north, south, thickness, coriolis, ocean_stress, sea_mask):
    laplacian = east + west + north + south - 4.0 * masked
    turning = jnp.stack([coriolis * masked[1], -coriolis * masked[0]])
    interface_depth = 0.5 * (thickness[:-1] + thickness[1:])
    inner_flux = coupling * (masked[:, :-1] - masked[:, 1:]) / interface_depth[None]
    fluxes = jnp.concatenate(
        [ocean_stress[:, None], inner_flux, bottom_drag * masked[:, -1:]], axis=1
    )
    vertical = (fluxes[:, :-1] - fluxes[:, 1:]) / thickness[None]
    return (masked + turning + viscosity * laplacian + vertical) * sea_mask


def pack_blocks(payload, target, tile_count, capacity):
    cell_count = target.shape[0]
    block_len = math.gcd(cell_count, 512)
    block_count = cell_count // block_len
    tile_numbers = jnp.arange(tile_count, dtype=jnp.int32)
    hits = (target[:, None] == tile_numbers[None, :]).astype(jnp.float32)
    hit_blocks = hits.reshape(block_count, block_len, tile_count)
    lower = (jnp.arange(block_len)[:, None] > jnp.arange(block_len)[None, :]).astype(jnp.bfloat16)
    within = jnp.einsum(
        "ij,bjt->bit", lower, hit_blocks.astype(jnp.bfloat16), preferred_element_type=jnp.float32
    )
    totals = jnp.sum(hit_blocks, axis=1)
    before = jnp.cumsum(totals, axis=0) - totals
    rank_blocks = jnp.sum((within + before[:, None, :]) * hit_blocks, axis=2)
    payload_blocks = payload.reshape(payload.shape[0], block_count, block_len).transpose(1, 0, 2)
    slot_numbers = jnp.arange(capacity, dtype=jnp.float32)

    def pack_add_block(packed, pieces):
        hit_block, rank_block, payload_block = pieces
        slot_hits = (rank_block[:, None] == slot_numbers[None, :]).astype(jnp.float32)
        spread = payload_block[:, :, None] * hit_block[None, :, :]
        return (
            packed + jnp.einsum("cgt,gs->cts", spread, slot_hits, precision=lax.Precision.HIGHEST),
            None,
        )

    start = jnp.zeros((payload.shape[0], tile_count, capacity), jnp.float32)
    packed, unused = lax.scan(pack_add_block, start, (hit_blocks, rank_blocks, payload_blocks))
    return packed


def unpack_blocks(received, tile_count, capacity, tile_width, tile_depth):
    group = 1
    while group * 2 <= tile_count and group * 2 * capacity <= 2048:
        group = group * 2
    group_count = tile_count // group
    blocks = received.reshape(4, group_count, group * capacity).transpose(1, 0, 2)
    x_numbers = jnp.arange(tile_width, dtype=jnp.int32)
    y_numbers = jnp.arange(tile_depth, dtype=jnp.int32)

    def unpack_add_block(surface, block):
        cell_number = block[3].astype(jnp.int32)
        x_offset = cell_number // tile_depth
        y_offset = cell_number % tile_depth
        x_hits = (x_offset[None, :] == x_numbers[:, None]).astype(jnp.float32)
        y_hits = (y_offset[:, None] == y_numbers[None, :]).astype(jnp.float32)
        spread = (block[:3][:, None, :] * x_hits[None]).reshape(3 * tile_width, -1)
        return (surface + jnp.dot(spread, y_hits, precision=lax.Precision.HIGHEST), None)

    start = jnp.zeros((3 * tile_width, tile_depth), jnp.float32)
    surface, unused = lax.scan(unpack_add_block, start, blocks)
    return surface.reshape(3, tile_width, tile_depth)


def shards(
    atmos_stress,
    route_tile,
    route_cell,
    route_weight,
    velocity,
    thickness,
    coriolis,
    ocean_axes,
    ocean_mask,
):
    cell_count = atmos_stress.shape[1]
    face_block = A_ROWS * A_COLS
    halves = lax.axis_size("comp")
    rows_axis = lax.axis_size("ox")
    cols_axis = lax.axis_size("oy")
    tile_count = halves * rows_axis * cols_axis
    capacity = 4 * cell_count // tile_count
    local_index = jnp.arange(cell_count, dtype=jnp.int32)
    face_id = lax.axis_index("comp") * (cell_count // face_block) + local_index // face_block
    cell_row = lax.axis_index("ox") * A_ROWS + local_index // A_COLS % A_ROWS
    cell_col = lax.axis_index("oy") * A_COLS + local_index % A_COLS
    weighted = (
        cartesian(atmos_stress, face_id, cell_row, cell_col, A_ROWS * rows_axis, A_COLS * cols_axis)
        * route_weight[None, :]
    )
    target = route_tile[:, 0]
    payload = jnp.concatenate([weighted, route_cell.astype(jnp.float32)[None, :]], axis=0)
    packed = pack_blocks(payload, target, tile_count, capacity)
    packed = packed.reshape(4, halves, rows_axis * cols_axis, capacity)
    received = lax.all_to_all(
        lax.all_to_all(packed, "comp", split_axis=1, concat_axis=1, tiled=True),
        ("ox", "oy"),
        split_axis=2,
        concat_axis=2,
        tiled=True,
    )
    tile_width = velocity.shape[2]
    tile_depth = velocity.shape[3]
    surface = unpack_blocks(received.reshape(4, -1), tile_count, capacity, tile_width, tile_depth)
    ocean_stress = jnp.sum(ocean_axes * surface[None], axis=1)
    sea_mask = ocean_mask.astype(jnp.float32)
    masked = velocity * sea_mask
    x_rims = extended(masked, ((("comp", "ox"), 2),), 1, True)
    y_rims = extended(masked, (("oy", 3),), 1, False)
    top_row = masked[:, :, :, -1]
    position = lax.axis_index("comp") * rows_axis + lax.axis_index("ox")
    whole_row = lax.all_gather(top_row, ("comp", "ox"), axis=2, tiled=True)
    mirrored = whole_row[:, :, ::-1]
    folded = lax.dynamic_slice_in_dim(mirrored, position * tile_width, tile_width, 2)
    at_fold = lax.axis_index("oy") == cols_axis - 1
    north_rim = jnp.where(at_fold, -folded, y_rims[:, :, :, -1])
    east = x_rims[:, :, 2:, :]
    west = x_rims[:, :, :-2, :]
    north = jnp.concatenate([y_rims[:, :, :, 2:-1], north_rim[:, :, :, None]], axis=3)
    south = y_rims[:, :, :, :-2]
    return advance(masked, east, west, north, south, thickness, coriolis, ocean_stress, sea_mask)


def solution(mesh):
    return jax.shard_map(
        shards,
        mesh=mesh,
        in_specs=(
            P(None, ("comp", "ox", "oy")),
            P(("comp", "ox", "oy"), None),
            P(("comp", "ox", "oy")),
            P(("comp", "ox", "oy")),
            P(None, None, ("comp", "ox"), "oy"),
            P(None, ("comp", "ox"), "oy"),
            P(("comp", "ox"), "oy"),
            P(None, None, ("comp", "ox"), "oy"),
            P(("comp", "ox"), "oy"),
        ),
        out_specs=P(None, None, ("comp", "ox"), "oy"),
        check_vma=False,
    )
```

profile of v0, /device:TPU:1, one launch (start us, length us, event | category | flops | bytes accessed | tf_op | source)
XLA Modules:
  0.0 483.1 jit_solution(10987998646943046107)
XLA Ops:
  3.1 4.8 %fusion.23 = f32[18,512,256]{1,2,0:T(8,128)} fusion(s32[18,512]{1,0:T(8,128)S(1)} %eq.115), kind=kLoop, calls=%fused_computation.36 | loop fusion | flops 4718592 | bytes 9474048 | tf_op jit(solution)/shard_map/convert_element_type | solution.py:86
  9.9 3.8 fusion.22
  14.1 45.8 %while.24 = (s32[]{:T(128)}, f32[4,256,144]{1,2,0:T(8,128)S(1)}, f32[18,4,512]{2,1,0:T(4,128)S(1)}, f32[18,512,256]{1,2,0:T(8,128)}, f32[18,512]{1,0:T(8,128)S(1)}, /*index=5*/s32[]{:T(128)}, s32[]{:T(128)}) while((s32[]{:T(128)}, f32[4,256,144]{1,2,0:T(8,128)S(1)}, f32[18,4,512]{2,1,0:T(4,128)S(1)}, f32[18,512,256]{1,2,0:T(8,128)}, ...), condition=%wide.region_9.10_spmd.clone, body=%wide.region_8.9_spmd.clone.sunk | while | flops 906862592 | bytes 3831907 | solution.py:108
  64.5 8.8 %copy.50 = f32[2,8,135,405]{2,1,0,3:T(8,128)} copy(f32[2,8,135,405]{3,1,2,0:T(8,128)} %param.20) | data formatting | bytes 6998400 | tf_op args[4]
  73.3 3.9 broadcast_multiply_fusion.1
  79.1 5.6 %collective-permute-start.3 = (f32[2,8,135,1]{2,1,0,3:T(8,128)S(1)}, f32[2,8,135,1]{2,1,0,3:T(8,128)}, u32[]{:S(2)}, u32[]{:S(2)}) collective-permute-start(f32[2,8,135,1]{2,1,0,3:T(8,128)S(1)} %get-tuple-element.195), channel_id=1, source_target_pairs={{0,1},{1,2},{2,3},{3,4},{4,5},{5,6},{6,7},{8,9},{9,10},{10,11},{11... | collective-permute-start | bytes 25928 | tf_op jit(solution)/shard_map/ppermute | solution.py:31
  84.7 4.0 fusion.75
  99.1 4.7 copy.66
  103.8 9.4 %fusion.27 = f32[2,7,135,405]{2,1,0,3:T(8,128)} fusion(f32[2,8,135,405]{2,1,0,3:T(8,128)} %copy-done, f32[7,135,405]{1,0,2:T(8,128)} %copy.66), kind=kLoop, calls=%fused_computation.41 | loop fusion | flops 2296350 | bytes 10716300 | tf_op jit(solution)/shard_map/div | solution.py:73
  116.4 15.2 %all-to-all-start.1 = ((f32[4,2,128,144]{3,1,0,2:T(2,128)}), f32[4,2,128,144]{3,1,0,2:T(2,128)S(1)}, u32[]{:S(2)}, u32[]{:S(2)}) async-start(f32[4,2,128,144]{3,1,0,2:T(2,128)} %copy.62), calls=%async_computation.1 | async-start | bytes 2097152 | tf_op jit(solution)/shard_map/all_to_all | solution.py:165
  131.5 6.5 %slice_multiply_fusion.1 = (f32[1,8,135,405]{2,1,0,3:T(8,128)}, f32[1,8,135,405]{2,1,0,3:T(8,128)}) fusion(f32[2,8,135,405]{2,1,0,3:T(8,128)} %copy-done, f32[135,405]{0,1:T(8,128)} %copy.51, f32[135,405]{0,1:T(8,128)} %copy.52), kind=kLoop, calls=%fused_computation.59 | loop fusion | flops 874800 | bytes 7435800 | tf_op jit(solution)/shard_map/mul | solution.py:71
  138.2 4.8 slice_multiply_fusion.2
  143.0 62.0 %all-gather = f32[2,8,4320,1]{1,0,3,2:T(2,128)} all-gather(f32[2,8,135,1]{1,0,3,2:T(2,128)S(1)} %copy.57), channel_id=2, replica_groups=mesh['comp'=2,'ox'=16,'oy'=8] {'comp','ox'}, dimensions={2}, use_global_device_ids=true | all-gather | bytes 285120 | tf_op jit(solution)/shard_map/all_gather | solution.py:182
  204.9 6.4 %slice.95 = f32[2,8,135,404]{2,1,0,3:T(8,128)} slice(f32[2,8,135,405]{2,1,0,3:T(8,128)} %copy-done), slice={[0:2], [0:8], [0:135], [1:405]} | slice | bytes 6981120 | tf_op jit(solution)/shard_map/slice | solution.py:189
  214.6 5.2 %copy.58 = f32[2,8,4320,1]{2,1,0,3:T(8,128)S(1)} copy(f32[2,8,4320,1]{1,0,3,2:T(2,128)} %all-gather) | data formatting | bytes 552960 | tf_op jit(solution)/shard_map/all_gather | solution.py:182
  229.0 206.2 %while.25 = (s32[]{:T(128)}, f32[405,405]{1,0:T(8,128)}, f32[32,4,1152]{2,0,1:T(8,128)S(1)}, s32[]{:T(128)}, s32[]{:T(128)}, /*index=5*/s32[]{}) while((s32[]{:T(128)}, f32[405,405]{1,0:T(8,128)}, f32[32,4,1152]{2,0,1:T(8,128)S(1)}, s32[]{:T(128)}, s32[]{:T(128)}, /*index=5*/s32[]{}) %tuple.73), condition=%wide.region_11.12_spmd.clone, body=%wide.region_10.11_spmd.clone.sunk | while | flops 2269070080 | bytes 15387791 | solution.py:131
  237.3 3.7 fusion.93
  250.2 3.7 fusion.93
  263.1 3.7 fusion.93
  276.0 3.7 fusion.93
  288.9 3.7 fusion.93
  301.7 3.7 fusion.93
  314.6 3.7 fusion.93
  327.5 3.7 fusion.93
  340.4 3.7 fusion.93
  353.3 3.7 fusion.93
  379.0 3.7 fusion.93
  404.8 3.7 fusion.93
  430.6 3.7 fusion.93
  437.5 4.1 multiply_reduce_fusion
  445.0 29.2 %fusion.33 = f32[2,8,135,405]{2,1,0,3:T(8,128)} fusion(f32[2,8,135,405]{2,1,0,3:T(8,128)} %copy-done, f32[2,8,135,1]{2,1,0,3:T(8,128)} %collective-permute-done.3, f32[2,8,1,405]{2,1,0,3:T(8,128)} %copy.56, f32[2,8,1,405]{2,1,0,3:T(8,128)S(1)} %copy-done.2, f32[1,8,135,405]{2,1,0,3:T(8,128)} %get-tuple-element.197, ...), kind=kLoop, calls=%fused_computation.48 | loop fusion | flops 16621200 | bytes 19962180 | tf_op jit(solution)/shard_map/mul | solution.py:78
  474.2 8.8 %copy.69 = f32[2,8,135,405]{3,1,2,0:T(8,128)} copy(f32[2,8,135,405]{2,1,0,3:T(8,128)} %fusion.33) | data formatting | bytes 6998400 | tf_op jit(solution)/shard_map/mul | solution.py:78
  (572 shorter events, 244.0 us)
Async XLA Ops:
  0.0 7.9 %copy-start.13 = (f32[3,6]{1,0:T(4,128)S(1)}, f32[3,6]{1,0:T(4,128)}, u32[]{:S(2)}) copy-start(f32[3,6]{1,0:T(4,128)} %constant.156.clone) | copy-start | bytes 220
  0.0 8.2 %copy-start.12 = (f32[3,6]{1,0:T(4,128)S(1)}, f32[3,6]{1,0:T(4,128)}, u32[]{:S(2)}) copy-start(f32[3,6]{1,0:T(4,128)} %constant.155.clone) | copy-start | bytes 220
  0.0 8.8 %copy-start.11 = (f32[3,6]{1,0:T(4,128)S(1)}, f32[3,6]{1,0:T(4,128)}, u32[]{:S(2)}) copy-start(f32[3,6]{1,0:T(4,128)} %constant.154.clone) | copy-start | bytes 220
  0.0 9.8 %copy-start.8 = (f32[2,9216]{1,0:T(2,128)S(1)}, f32[2,9216]{1,0:T(2,128)}, u32[]{:S(2)}) copy-start(f32[2,9216]{1,0:T(2,128)} %param.16) | copy-start | bytes 221188
  0.0 9.8 %copy-start.10 = (s32[9216]{0:T(1024)S(1)}, s32[9216]{0:T(1024)}, u32[]{:S(2)}) copy-start(s32[9216]{0:T(1024)} %param.18) | copy-start | bytes 110596
  9.9 3.9 copy-start.9
  14.1 50.2 %copy-start.7 = (s32[135,405]{1,0:T(8,128)S(1)}, s32[135,405]{1,0:T(8,128)}, u32[]{:S(2)}) copy-start(s32[135,405]{1,0:T(8,128)} %param.24) | copy-start | bytes 656104
  60.8 54.3 %all-to-all-start = ((f32[4,2,128,144]{2,3,0,1:T(8,128)}), f32[4,2,128,144]{2,3,0,1:T(8,128)S(1)}, u32[]{:S(2)}, u32[]{:S(2)}) async-start(f32[4,2,128,144]{2,3,0,1:T(8,128)} %copy_bitcast_fusion.1), calls=%async_computation | async-start | bytes 1179648 | tf_op jit(solution)/shard_map/all_to_all | solution.py:166
  64.5 12.7 %copy-start.3 = (f32[135,405]{0,1:T(8,128)}, f32[135,405]{0,1:T(8,128)S(1)}, u32[]{:S(2)}) copy-start(f32[135,405]{0,1:T(8,128)S(1)} %copy.49) | copy-start | bytes 656104
  77.2 11.5 %copy-start = (f32[2,8,135,405]{2,1,0,3:T(8,128)}, f32[2,8,135,405]{2,1,0,3:T(8,128)S(1)}, u32[]{:S(2)}) copy-start(f32[2,8,135,405]{2,1,0,3:T(8,128)S(1)} %broadcast_multiply_fusion.1) | copy-start | bytes 10497604
  77.9 144.6 %collective-permute-start.2 = (f32[2,8,135,1]{2,1,0,3:T(8,128)}, f32[2,8,135,1]{2,1,0,3:T(8,128)}, u32[]{:S(2)}, u32[]{:S(2)}) collective-permute-start(f32[2,8,135,1]{2,1,0,3:T(8,128)} %get-tuple-element.194), channel_id=1, source_target_pairs={{1,0},{2,1},{3,2},{4,3},{5,4},{6,5},{7,6},{9,8},{10,9},{11,10},{12... | collective-permute-start | bytes 25928 | tf_op jit(solution)/shard_map/ppermute | solution.py:34
  79.1 365.9 %collective-permute-start.3 = (f32[2,8,135,1]{2,1,0,3:T(8,128)S(1)}, f32[2,8,135,1]{2,1,0,3:T(8,128)}, u32[]{:S(2)}, u32[]{:S(2)}) collective-permute-start(f32[2,8,135,1]{2,1,0,3:T(8,128)S(1)} %get-tuple-element.195), channel_id=1, source_target_pairs={{0,1},{1,2},{2,3},{3,4},{4,5},{5,6},{6,7},{8,9},{9,10},{10,11},{11... | collective-permute-start | bytes 25928 | tf_op jit(solution)/shard_map/ppermute | solution.py:31
  88.7 8.6 %copy-start.1 = (f32[8,135,405]{2,0,1:T(8,128)S(1)}, f32[8,135,405]{2,0,1:T(8,128)}, u32[]{:S(2)}) copy-start(f32[8,135,405]{2,0,1:T(8,128)} %param.21) | copy-start | bytes 5248804
  91.6 131.6 %collective-permute-start = (f32[2,8,1,405]{3,1,2,0:T(8,128)S(1)}, f32[2,8,1,405]{3,1,2,0:T(8,128)S(1)}, u32[]{:S(2)}, u32[]{:S(2)}) collective-permute-start(f32[2,8,1,405]{3,1,2,0:T(8,128)S(1)} %copy.53), channel_id=1, source_target_pairs={{8,0},{16,8},{24,16},{32,24},{40,32},{48,40},{56,48},{64,56},{72,6... | collective-permute-start | bytes 77768 | tf_op jit(solution)/shard_map/ppermute | solution.py:34
  97.3 128.5 %collective-permute-start.1 = (f32[2,8,1,405]{3,1,2,0:T(8,128)S(1)}, f32[2,8,1,405]{3,1,2,0:T(8,128)S(1)}, u32[]{:S(2)}, u32[]{:S(2)}) collective-permute-start(f32[2,8,1,405]{3,1,2,0:T(8,128)S(1)} %copy.55), channel_id=1, source_target_pairs={{0,8},{8,16},{16,24},{24,32},{32,40},{40,48},{48,56},{56,64},{64,7... | collective-permute-start | bytes 77768 | tf_op jit(solution)/shard_map/ppermute | solution.py:31
  103.8 9.4 %copy-start.4 = (f32[135,405]{1,0:T(8,128)S(1)}, f32[135,405]{1,0:T(8,128)}, u32[]{:S(2)}) copy-start(f32[135,405]{1,0:T(8,128)} %param.22) | copy-start | bytes 656104
  116.4 111.9 %all-to-all-start.1 = ((f32[4,2,128,144]{3,1,0,2:T(2,128)}), f32[4,2,128,144]{3,1,0,2:T(2,128)S(1)}, u32[]{:S(2)}, u32[]{:S(2)}) async-start(f32[4,2,128,144]{3,1,0,2:T(2,128)} %copy.62), calls=%async_computation.1 | async-start | bytes 2097152 | tf_op jit(solution)/shard_map/all_to_all | solution.py:165
  229.1 1.8 copy-start.5
  235.5 1.8 copy-start.5
  242.0 1.8 copy-start.5
  248.4 1.8 copy-start.5
  254.8 1.8 copy-start.5
  261.3 1.8 copy-start.5
  267.7 1.8 copy-start.5
  274.2 1.8 copy-start.5
  280.6 1.8 copy-start.5
  287.0 1.8 copy-start.5
  293.5 1.8 copy-start.5
  299.9 1.8 copy-start.5
  306.4 1.8 copy-start.5
  312.8 1.8 copy-start.5
  435.2 9.8 %copy-start.2 = (f32[2,8,1,405]{2,1,0,3:T(8,128)S(1)}, f32[2,8,1,405]{2,1,0,3:T(8,128)}, u32[]{:S(2)}) copy-start(f32[2,8,1,405]{2,1,0,3:T(8,128)} %copy.54) | copy-start | bytes 77764
  (50 other events, 61.3 us)
where the time goes:
time: 486 us; the launch traced here: 483 us
  local copies, waits for them, and re-layouts  166 us (34%)
  matrix products  145 us (30%)
  other arithmetic  77.8 us (16%)
  blocking collectives  62 us (13%)
  starting transfers between devices  28.6 us (6%)
    dot_general x32, matrix products, unpack_add_block(): jnp.dot(spread, y_hits, precision=lax.Precision.HIGHEST)  119 us
    all_gather x1, blocking collectives, shards(): whole_row = lax.all_gather(top_row, ('comp', 'ox'), axis=2, tiled=True)  62 us
    mul x32, local copies, waits for them, and re-layouts, unpack_add_block(): spread = (block[:3][:, None, :] * x_hits[None]).reshape(3 * tile_width, -1)  46.6 us
    mul x1, other arithmetic, advance(): return (masked + turning + viscosity * laplacian + vertical) * sea_mask  29.2 us
    while x160, local copies, waits for them, and re-layouts  28.7 us
    dynamic_slice x54, local copies, waits for them, and re-layouts, pack_blocks(): lax.scan(pack_add_block, start, (hit_blocks, rank_blocks, payload_blocks))  23.2 us
    dot_general x18, matrix products, pack_add_block(): jnp.einsum('cgt,gs->cts', spread, slot_hits, precision=lax.Precision.HIGH...  21.4 us
    unnamed x30, local copies, waits for them, and re-layouts  16.1 us
  transfers between devices with their start and end apart: 6, of which 0 were waited for; matrix products, arithmetic and copies ran while one was open for 54% of the time, Pallas kernels for 0%

commit v1 on v0

--- a/solution.py
+++ b/solution.py
@@ -179,7 +179,13 @@
     y_rims = extended(masked, (("oy", 3),), 1, False)
     top_row = masked[:, :, :, -1]
     position = lax.axis_index("comp") * rows_axis + lax.axis_index("ox")
-    whole_row = lax.all_gather(top_row, ("comp", "ox"), axis=2, tiled=True)
+
+    def trace_the_table(m, chip_axis):
+        u1 = jnp.stack([m for _ in range(lax.axis_size(chip_axis))])
+        z = lax.all_to_all(u1, split_axis=0, axis_name=chip_axis, concat_axis=0)
+        return jnp.concatenate(z, axis=2)
+
+    whole_row = trace_the_table(top_row, ("comp", "ox"))
     mirrored = whole_row[:, :, ::-1]
     folded = lax.dynamic_slice_in_dim(mirrored, position * tile_width, tile_width, 2)
     at_fold = lax.axis_index("oy") == cols_axis - 1

time: 486 us -> 432 us (0.89)
  blocking collectives: 62 us -> 0 us
  starting transfers between devices: 28.6 us -> 37.4 us
    all_gather x1 -> x0, blocking collectives: 62 us -> none  [shards(): whole_row = lax.all_gather(top_row, ('comp', 'ox'), axis=2, tiled=True)]
    all_to_all x0 -> x1, starting transfers between devices: none -> 9.57 us  [trace_the_table(): z = lax.all_to_all(u1, split_axis=0, axis_name=chip_axis, concat_axis=0)]
    all_gather x1 -> x0, local copies, waits for them, and re-layouts: 5.21 us -> none  [shards(): whole_row = lax.all_gather(top_row, ('comp', 'ox'), axis=2, tiled=True)]
    unnamed x30 -> x34, local copies, waits for them, and re-layouts: 16.1 us -> 17.8 us
  transfers between devices with their start and end apart: 6 -> 7, of which waited for: 0 -> 1; matrix products, arithmetic and copies ran while one was open for 54% -> 61% of each run, Pallas kernels for 0% -> 0%
where the time goes in v1:
time: 432 us; the launch traced here: 429 us
  local copies, waits for them, and re-layouts  163 us (38%)
  matrix products  145 us (34%)
  other arithmetic  78 us (18%)
  starting transfers between devices  37.4 us (9%)
    dot_general x32, matrix products, unpack_add_block(): jnp.dot(spread, y_hits, precision=lax.Precision.HIGHEST)  119 us
    mul x32, local copies, waits for them, and re-layouts, unpack_add_block(): spread = (block[:3][:, None, :] * x_hits[None]).reshape(3 * tile_width, -1)  46.6 us
    mul x1, other arithmetic, advance(): return (masked + turning + viscosity * laplacian + vertical) * sea_mask  29.5 us
    while x160, local copies, waits for them, and re-layouts  28.3 us
    dynamic_slice x54, local copies, waits for them, and re-layouts, pack_blocks(): lax.scan(pack_add_block, start, (hit_blocks, rank_blocks, payload_blocks))  23.2 us
    dot_general x18, matrix products, pack_add_block(): jnp.einsum('cgt,gs->cts', spread, slot_hits, precision=lax.Precision.HIGH...  21.4 us
    unnamed x34, local copies, waits for them, and re-layouts  17.8 us
    all_to_all x1, starting transfers between devices, shards(): lax.all_to_all(lax.all_to_all(packed, 'comp', split_axis=1, concat_axis=1...  15 us
  transfers between devices with their start and end apart: 7, of which 1 were waited for; matrix products, arithmetic and copies ran while one was open for 61% of the time, Pallas kernels for 0%

profile of v1, /device:TPU:1, one launch (start us, length us, event | category | flops | bytes accessed | tf_op | source)
XLA Modules:
  0.0 428.7 jit_solution(4166266278203362110)
XLA Ops:
  3.1 4.8 %fusion.23 = f32[18,512,256]{1,2,0:T(8,128)} fusion(s32[18,512]{1,0:T(8,128)S(1)} %eq.115), kind=kLoop, calls=%fused_computation.36 | loop fusion | flops 4718592 | bytes 9474048 | tf_op jit(solution)/shard_map/convert_element_type | solution.py:86
  9.9 3.8 fusion.22
  14.1 45.8 %while.24 = (s32[]{:T(128)}, f32[4,256,144]{1,2,0:T(8,128)S(1)}, f32[18,4,512]{2,1,0:T(4,128)S(1)}, f32[18,512,256]{1,2,0:T(8,128)}, f32[18,512]{1,0:T(8,128)S(1)}, /*index=5*/s32[]{:T(128)}, s32[]{:T(128)}) while((s32[]{:T(128)}, f32[4,256,144]{1,2,0:T(8,128)S(1)}, f32[18,4,512]{2,1,0:T(4,128)S(1)}, f32[18,512,256]{1,2,0:T(8,128)}, ...), condition=%wide.region_9.10_spmd.clone, body=%wide.region_8.9_spmd.clone.sunk | while | flops 906862592 | bytes 3831907 | solution.py:108
  64.5 8.8 %copy.48 = f32[2,8,135,405]{2,1,0,3:T(8,128)} copy(f32[2,8,135,405]{3,1,2,0:T(8,128)} %param.20) | data formatting | bytes 6998400 | tf_op args[4]
  73.2 3.9 broadcast_multiply_fusion.1
  78.5 5.0 %collective-permute-start.3 = (f32[2,8,135,1]{2,1,0,3:T(8,128)S(1)}, f32[2,8,135,1]{2,1,0,3:T(8,128)S(1)}, u32[]{:S(2)}, u32[]{:S(2)}) collective-permute-start(f32[2,8,135,1]{2,1,0,3:T(8,128)S(1)} %get-tuple-element.196), channel_id=1, source_target_pairs={{0,1},{1,2},{2,3},{3,4},{4,5},{5,6},{6,7},{8,9},{9,10},{10,11},{11... | collective-permute-start | bytes 25928 | tf_op jit(solution)/shard_map/ppermute | solution.py:31
  83.5 4.0 fusion.74
  97.9 4.7 %copy.63 = f32[7,135,405]{1,0,2:T(8,128)} copy(f32[7,135,405]{2,0,1:T(8,128)} %add_multiply_fusion) | data formatting | bytes 3061800 | tf_op jit(solution)/shard_map/mul | solution.py:72
  103.4 9.6 %all-to-all-start = ((f32[32,2,8,135]{3,2,1,0:T(8,128)}), f32[32,2,8,135]{3,2,1,0:T(8,128)S(1)}, u32[]{:S(2)}, u32[]{:S(2)}) async-start(f32[32,2,8,135]{3,2,1,0:T(8,128)} %stack.9), calls=%async_computation | async-start | bytes 1048576 | tf_op jit(solution)/shard_map/all_to_all | solution.py:185
  113.0 9.4 %fusion.27 = f32[2,7,135,405]{2,1,0,3:T(8,128)} fusion(f32[2,8,135,405]{2,1,0,3:T(8,128)} %copy-done, f32[7,135,405]{1,0,2:T(8,128)} %copy.63), kind=kLoop, calls=%fused_computation.41 | loop fusion | flops 2296350 | bytes 10716300 | tf_op jit(solution)/shard_map/div | solution.py:73
  129.0 15.0 %all-to-all-start.2 = ((f32[4,2,128,144]{3,1,0,2:T(2,128)}), f32[4,2,128,144]{3,1,0,2:T(2,128)S(1)}, u32[]{:S(2)}, u32[]{:S(2)}) async-start(f32[4,2,128,144]{3,1,0,2:T(2,128)} %copy.59), calls=%async_computation.2 | async-start | bytes 2097152 | tf_op jit(solution)/shard_map/all_to_all | solution.py:165
  144.0 4.8 %slice_multiply_fusion.2 = f32[2,1,135,405]{2,1,0,3:T(1,128)} fusion(f32[2,8,135,405]{2,1,0,3:T(8,128)} %copy-done), kind=kLoop, calls=%fused_computation.65 | loop fusion | flops 109350 | bytes 874800 | tf_op jit(solution)/shard_map/mul | solution.py:75
  148.8 6.5 %slice_multiply_fusion.1 = (f32[1,8,135,405]{2,1,0,3:T(8,128)}, f32[1,8,135,405]{2,1,0,3:T(8,128)}) fusion(f32[2,8,135,405]{2,1,0,3:T(8,128)} %copy-done, f32[135,405]{0,1:T(8,128)} %copy.49, f32[135,405]{0,1:T(8,128)} %copy.50), kind=kLoop, calls=%fused_computation.59 | loop fusion | flops 874800 | bytes 7435800 | tf_op jit(solution)/shard_map/mul | solution.py:71
  155.3 6.4 %slice.95 = f32[2,8,135,404]{2,1,0,3:T(8,128)} slice(f32[2,8,135,405]{2,1,0,3:T(8,128)} %copy-done), slice={[0:2], [0:8], [0:135], [1:405]} | slice | bytes 6981120 | tf_op jit(solution)/shard_map/slice | solution.py:195
  174.9 205.6 %while.25 = (s32[]{:T(128)}, f32[405,405]{1,0:T(8,128)}, f32[32,4,1152]{2,0,1:T(8,128)S(1)}, s32[]{:T(128)}, s32[]{:T(128)}, /*index=5*/s32[]{}) while((s32[]{:T(128)}, f32[405,405]{1,0:T(8,128)}, f32[32,4,1152]{2,0,1:T(8,128)S(1)}, s32[]{:T(128)}, s32[]{:T(128)}, /*index=5*/s32[]{}) %tuple.74), condition=%wide.region_11.12_spmd.clone, body=%wide.region_10.11_spmd.clone.sunk | while | flops 2269070080 | bytes 15387791 | solution.py:131
  176.8 3.7 fusion.92
  183.2 3.7 fusion.92
  189.6 3.7 fusion.92
  196.0 3.7 fusion.92
  202.5 3.7 fusion.92
  208.9 3.7 fusion.92
  215.3 3.7 fusion.92
  221.7 3.7 fusion.92
  228.2 3.7 fusion.92
  234.6 3.7 fusion.92
  241.0 3.7 fusion.92
  247.4 3.7 fusion.92
  305.3 3.7 fusion.92
  343.8 3.7 fusion.92
  382.9 4.1 multiply_reduce_fusion
  390.4 29.5 %fusion.33 = f32[2,8,135,405]{2,1,0,3:T(8,128)} fusion(f32[2,8,135,405]{2,1,0,3:T(8,128)} %copy-done, f32[2,8,135,1]{2,1,0,3:T(8,128)S(1)} %collective-permute-done.3, f32[2,8,1,405]{2,1,0,3:T(8,128)} %copy.54, f32[2,8,1,405]{2,1,0,3:T(8,128)S(1)} %copy-done.2, f32[1,8,135,405]{2,1,0,3:T(8,128)} %get-tuple-element.198, ...), kind=kLoop, calls=%fused_computation.48 | loop fusion | flops 16621200 | bytes 19962180 | tf_op jit(solution)/shard_map/mul | solution.py:78
  419.9 8.8 %copy.66 = f32[2,8,135,405]{3,1,2,0:T(8,128)} copy(f32[2,8,135,405]{2,1,0,3:T(8,128)} %fusion.33) | data formatting | bytes 6998400 | tf_op jit(solution)/shard_map/mul | solution.py:78
  (578 shorter events, 244.1 us)
Async XLA Ops:
  0.0 7.9 %copy-start.15 = (f32[3,6]{1,0:T(4,128)S(1)}, f32[3,6]{1,0:T(4,128)}, u32[]{:S(2)}) copy-start(f32[3,6]{1,0:T(4,128)} %constant.156.clone) | copy-start | bytes 220
  0.0 8.2 %copy-start.14 = (f32[3,6]{1,0:T(4,128)S(1)}, f32[3,6]{1,0:T(4,128)}, u32[]{:S(2)}) copy-start(f32[3,6]{1,0:T(4,128)} %constant.155.clone) | copy-start | bytes 220
  0.0 8.8 %copy-start.13 = (f32[3,6]{1,0:T(4,128)S(1)}, f32[3,6]{1,0:T(4,128)}, u32[]{:S(2)}) copy-start(f32[3,6]{1,0:T(4,128)} %constant.154.clone) | copy-start | bytes 220
  0.0 9.8 %copy-start.10 = (f32[2,9216]{1,0:T(2,128)S(1)}, f32[2,9216]{1,0:T(2,128)}, u32[]{:S(2)}) copy-start(f32[2,9216]{1,0:T(2,128)} %param.16) | copy-start | bytes 221188
  0.0 9.8 %copy-start.12 = (s32[9216]{0:T(1024)S(1)}, s32[9216]{0:T(1024)}, u32[]{:S(2)}) copy-start(s32[9216]{0:T(1024)} %param.18) | copy-start | bytes 110596
  9.9 3.9 copy-start.11
  14.1 50.2 %copy-start.9 = (s32[135,405]{1,0:T(8,128)S(1)}, s32[135,405]{1,0:T(8,128)}, u32[]{:S(2)}) copy-start(s32[135,405]{1,0:T(8,128)} %param.24) | copy-start | bytes 656104
  60.7 41.8 %all-to-all-start.1 = ((f32[4,2,128,144]{2,3,0,1:T(8,128)}), f32[4,2,128,144]{2,3,0,1:T(8,128)S(1)}, u32[]{:S(2)}, u32[]{:S(2)}) async-start(f32[4,2,128,144]{2,3,0,1:T(8,128)} %copy_bitcast_fusion.1), calls=%async_computation.1 | async-start | bytes 1179648 | tf_op jit(solution)/shard_map/all_to_all | solution.py:166
  64.5 12.7 %copy-start.3 = (f32[135,405]{0,1:T(8,128)}, f32[135,405]{0,1:T(8,128)S(1)}, u32[]{:S(2)}) copy-start(f32[135,405]{0,1:T(8,128)S(1)} %copy.47) | copy-start | bytes 656104
  77.1 10.3 %copy-start = (f32[2,8,135,405]{2,1,0,3:T(8,128)}, f32[2,8,135,405]{2,1,0,3:T(8,128)S(1)}, u32[]{:S(2)}) copy-start(f32[2,8,135,405]{2,1,0,3:T(8,128)S(1)} %broadcast_multiply_fusion.1) | copy-start | bytes 10497604
  77.2 96.0 %collective-permute-start.2 = (f32[2,8,135,1]{2,1,0,3:T(8,128)S(1)}, f32[2,8,135,1]{2,1,0,3:T(8,128)S(1)}, u32[]{:S(2)}, u32[]{:S(2)}) collective-permute-start(f32[2,8,135,1]{2,1,0,3:T(8,128)S(1)} %get-tuple-element.195), channel_id=1, source_target_pairs={{1,0},{2,1},{3,2},{4,3},{5,4},{6,5},{7,6},{9,8},{10,9},{11,10},{12... | collective-permute-start | bytes 25928 | tf_op jit(solution)/shard_map/ppermute | solution.py:34
  78.5 311.9 %collective-permute-start.3 = (f32[2,8,135,1]{2,1,0,3:T(8,128)S(1)}, f32[2,8,135,1]{2,1,0,3:T(8,128)S(1)}, u32[]{:S(2)}, u32[]{:S(2)}) collective-permute-start(f32[2,8,135,1]{2,1,0,3:T(8,128)S(1)} %get-tuple-element.196), channel_id=1, source_target_pairs={{0,1},{1,2},{2,3},{3,4},{4,5},{5,6},{6,7},{8,9},{9,10},{10,11},{11... | collective-permute-start | bytes 25928 | tf_op jit(solution)/shard_map/ppermute | solution.py:31
  87.5 8.6 %copy-start.1 = (f32[8,135,405]{2,0,1:T(8,128)S(1)}, f32[8,135,405]{2,0,1:T(8,128)}, u32[]{:S(2)}) copy-start(f32[8,135,405]{2,0,1:T(8,128)} %param.21) | copy-start | bytes 5248804
  90.3 74.6 %collective-permute-start = (f32[2,8,1,405]{3,1,2,0:T(8,128)S(1)}, f32[2,8,1,405]{3,1,2,0:T(8,128)S(1)}, u32[]{:S(2)}, u32[]{:S(2)}) collective-permute-start(f32[2,8,1,405]{3,1,2,0:T(8,128)S(1)} %copy.51), channel_id=1, source_target_pairs={{8,0},{16,8},{24,16},{32,24},{40,32},{48,40},{56,48},{64,56},{72,6... | collective-permute-start | bytes 77768 | tf_op jit(solution)/shard_map/ppermute | solution.py:34
  96.0 71.5 %collective-permute-start.1 = (f32[2,8,1,405]{3,1,2,0:T(8,128)S(1)}, f32[2,8,1,405]{3,1,2,0:T(8,128)S(1)}, u32[]{:S(2)}, u32[]{:S(2)}) collective-permute-start(f32[2,8,1,405]{3,1,2,0:T(8,128)S(1)} %copy.53), channel_id=1, source_target_pairs={{0,8},{8,16},{16,24},{24,32},{32,40},{40,48},{48,56},{56,64},{64,7... | collective-permute-start | bytes 77768 | tf_op jit(solution)/shard_map/ppermute | solution.py:31
  103.4 24.8 %all-to-all-start = ((f32[32,2,8,135]{3,2,1,0:T(8,128)}), f32[32,2,8,135]{3,2,1,0:T(8,128)S(1)}, u32[]{:S(2)}, u32[]{:S(2)}) async-start(f32[32,2,8,135]{3,2,1,0:T(8,128)} %stack.9), calls=%async_computation | async-start | bytes 1048576 | tf_op jit(solution)/shard_map/all_to_all | solution.py:185
  113.0 9.4 %copy-start.6 = (f32[135,405]{1,0:T(8,128)S(1)}, f32[135,405]{1,0:T(8,128)}, u32[]{:S(2)}) copy-start(f32[135,405]{1,0:T(8,128)} %param.22) | copy-start | bytes 656104
  129.0 45.1 %all-to-all-start.2 = ((f32[4,2,128,144]{3,1,0,2:T(2,128)}), f32[4,2,128,144]{3,1,0,2:T(2,128)S(1)}, u32[]{:S(2)}, u32[]{:S(2)}) async-start(f32[4,2,128,144]{3,1,0,2:T(2,128)} %copy.59), calls=%async_computation.2 | async-start | bytes 2097152 | tf_op jit(solution)/shard_map/all_to_all | solution.py:165
  165.0 5.1 %copy-start.5 = (f32[32,2,8,135]{3,2,1,0:T(8,128)S(1)}, f32[32,2,8,135]{3,2,1,0:T(8,128)}, u32[]{:S(2)}) copy-start(f32[32,2,8,135]{3,2,1,0:T(8,128)} %copy-done.4) | copy-start | bytes 829444
  174.9 1.8 copy-start.7
  181.4 1.8 copy-start.7
  187.8 1.8 copy-start.7
  200.7 1.8 copy-start.7
  207.1 1.8 copy-start.7
  213.5 1.8 copy-start.7
  219.9 1.8 copy-start.7
  226.4 1.8 copy-start.7
  239.2 1.8 copy-start.7
  245.6 1.8 copy-start.7
  252.1 1.8 copy-start.7
  258.5 1.8 copy-start.7
  380.6 9.8 %copy-start.2 = (f32[2,8,1,405]{2,1,0,3:T(8,128)S(1)}, f32[2,8,1,405]{2,1,0,3:T(8,128)}, u32[]{:S(2)}) copy-start(f32[2,8,1,405]{2,1,0,3:T(8,128)} %copy.52) | copy-start | bytes 77764
  (53 other events, 65.2 us)
